TPU v7x, 32 devices: a whole 2x2x4 slice. The times are simulated.
32 devices in a mesh: groups: 2 (over y), tm: 4 (over z), band: 2 (over x), tmpl: 2 (over core).
Axes of the slice: x: 2, y: 2, z: 4, core: 2. Of those that a mesh axis runs over, the one named last changes fastest.
Arguments:
- sft_bins: float32 [2, 128, 2048], P(None, ('groups', 'tm'), 'band'), parts along dimension 1, may hold values from -6 to 6
- delay_code: int32 [8, 128, 1024], P(('groups', 'tmpl'), None, ('tm', 'band')), parts along dimension 0, may hold values from 0 to 16007, as said below
- antenna: float32 [8, 2, 128, 1024], P(('groups', 'tmpl'), None, None, ('tm', 'band')), parts along dimension 0, may hold values from -10 to 10
Outputs:
- f_stat: float32 [8, 128, 8, 128], P(('groups', 'tmpl'), None, ('tm', 'band')), parts along dimension 0
There are 2 independent parts, one for each index of `groups`. A program takes and returns all parts, laid end to end along the dimension named above; each array names one. Nothing has to cross between parts.
Inputs may be any that keep to these rules, and one draw needn't show every extreme that they name: `delay_code`: the whole delay o of a template is the same for all samples n of each aligned run of 256 samples (n // 256 equal).
All inputs are finite; a program needn't handle non-finite values.
Results may differ from a plain program's by a relative error of at most 0.0003.
Values sent between devices are 32-bit elements; how exact they have to be, the bound alone decides.
No kernel may reach another device: no remote copies, remote signals or barrier semaphores. Data moves between devices by JAX's collectives and lax.ppermute only.
A program may use at most 64 MiB of HBM per device.

v0:
```python
import math
import jax
import jax.numpy as jnp
from jax import lax
from jax.sharding import PartitionSpec as P

NB = 2048
NQ = 128
NP = 16
SFT_DEV = 8
MAXD = 1000
NFRAC = 8
RUN = 256
stat_eps = 1e-06
floor_share = 0.5


def shifted(value, axis, by):
    length = lax.axis_size(axis)
    pairs = [(i, i + by) for i in range(length) if 0 <= i + by < length]
    return lax.ppermute(value, axis, pairs)


def lagrange(fraction):
    return (
        -fraction * (fraction - 1.0) * (fraction - 2.0) / 6.0,
        (fraction + 1.0) * (fraction - 1.0) * (fraction - 2.0) / 2.0,
        -(fraction + 1.0) * fraction * (fraction - 2.0) / 2.0,
        (fraction + 1.0) * fraction * (fraction - 1.0) / 6.0,
    )


def phase_pair(product, modulus, direction):
    angles = direction * 2.0 * math.pi / modulus * (product % modulus).astype(jnp.float32)
    return (jnp.cos(angles), jnp.sin(angles))


def dft_table(length, direction):
    rows_at = lax.broadcasted_iota(jnp.int32, (length, length), 0)
    cols_at = lax.broadcasted_iota(jnp.int32, (length, length), 1)
    return phase_pair(rows_at * cols_at, length, direction)


def complex_einsum(pattern, lhs_pair, rhs_pair):
    lhs_real, lhs_imag = lhs_pair
    rhs_real, rhs_imag = rhs_pair
    high = lax.Precision.HIGHEST
    out_real = jnp.einsum(pattern, lhs_real, rhs_real, precision=high) - jnp.einsum(
        pattern, lhs_imag, rhs_imag, precision=high
    )
    out_imag = jnp.einsum(pattern, lhs_real, rhs_imag, precision=high) + jnp.einsum(
        pattern, lhs_imag, rhs_real, precision=high
    )
    return (out_real, out_imag)


def rotate(values, phases):
    val_real, val_imag = values
    cos_part, sin_part = phases
    return (val_real * cos_part - val_imag * sin_part, val_real * sin_part + val_imag * cos_part)


def apply_weights(arrived):
    return arrived[:, 1][:, :, None] * arrived[:, 0][:, None]


def finish(arrived):
    owners = lax.axis_size("tm") * lax.axis_size("band")
    my_rank = lax.axis_index("tm") * lax.axis_size("band") + lax.axis_index("band")
    q_local = arrived.shape[3]
    lane_width = arrived.shape[5]
    sample_total = SFT_DEV * owners * NB
    section_one = complex_einsum(
        "abqix,ic->abqcx", (arrived[:, :, 0], arrived[:, :, 1]), dft_table(owners, -1.0)
    )
    c_pos = lax.broadcasted_iota(jnp.int32, (owners, lane_width), 0)
    x_pos = lax.broadcasted_iota(jnp.int32, (owners, lane_width), 1)
    section_one = rotate(section_one, phase_pair(c_pos * (x_pos // NP), SFT_DEV * owners, -1.0))
    short_table = dft_table(SFT_DEV, -1.0)
    ident_rows = jnp.eye(NP, dtype=jnp.float32)
    spread = (jnp.kron(short_table[0], ident_rows), jnp.kron(short_table[1], ident_rows))
    section_two = complex_einsum("abqcx,xy->abqcy", section_one, spread)
    q_grid = my_rank * q_local + lax.broadcasted_iota(jnp.int32, (q_local, owners, lane_width), 0)
    c_grid = lax.broadcasted_iota(jnp.int32, (q_local, owners, lane_width), 1)
    x_grid = lax.broadcasted_iota(jnp.int32, (q_local, owners, lane_width), 2)
    time_index = x_grid % NP + NP * q_grid
    freq_index = c_grid + owners * (x_grid // NP)
    section_two = rotate(section_two, phase_pair(time_index * freq_index, sample_total, -1.0))
    packed = jnp.stack(section_two, axis=2)
    turned = lax.all_to_all(packed, ("tm", "band"), split_axis=4, concat_axis=3, tiled=True)
    turned = turned.reshape(turned.shape[0], 2, 2, NQ, lane_width)
    section_three = complex_einsum(
        "abqx,qv->abvx", (turned[:, :, 0], turned[:, :, 1]), dft_table(NQ, -1.0)
    )
    v_pos = lax.broadcasted_iota(jnp.int32, (NQ, lane_width), 0)
    p_pos = lax.broadcasted_iota(jnp.int32, (NQ, lane_width), 1) % NP
    section_three = rotate(section_three, phase_pair(v_pos * p_pos, NB, -1.0))
    fine_table = dft_table(NP, -1.0)
    ident_blocks = jnp.eye(SFT_DEV, dtype=jnp.float32)
    block_table = (jnp.kron(ident_blocks, fine_table[0]), jnp.kron(ident_blocks, fine_table[1]))
    result = complex_einsum("abvx,xy->abvy", section_three, block_table)
    return jnp.stack(result, axis=2)


def per_device(sft_bins, delay_code, antenna):
    owners = lax.axis_size("tm") * lax.axis_size("band")
    sample_total = SFT_DEV * owners * NB
    spectra = lax.all_to_all(sft_bins, "band", split_axis=1, concat_axis=2, tiled=True)
    bin_grid = spectra.reshape(2, SFT_DEV, NP, NQ)
    section_one = complex_einsum("pk,skl->spl", dft_table(NP, 1.0), (bin_grid[0], bin_grid[1]))
    p_rows = lax.broadcasted_iota(jnp.int32, (NP, NQ), 0)
    l_cols = lax.broadcasted_iota(jnp.int32, (NP, NQ), 1)
    section_one = rotate(section_one, phase_pair(p_rows * l_cols, NB, 1.0))
    series_pair = complex_einsum("spl,lq->spq", section_one, dft_table(NQ, 1.0))
    norm_scale = 1.0 / math.sqrt(NB)
    stacked = jnp.stack([series_pair[0] * norm_scale, series_pair[1] * norm_scale])
    rim_cols = (MAXD + 1 + NP) // NP
    head_rim = stacked[:, 0, :, :rim_cols]
    tail_rim = stacked[:, SFT_DEV - 1, :, NQ - rim_cols :]
    after_rim = shifted(head_rim, ("tm", "band"), -1)
    before = shifted(tail_rim, ("tm", "band"), 1)
    rim_size = NP * rim_cols
    span_len = SFT_DEV * NB
    timed = stacked.transpose(0, 1, 3, 2).reshape(2, span_len)
    before_timed = before.transpose(0, 2, 1).reshape(2, rim_size)
    after_timed = after_rim.transpose(0, 2, 1).reshape(2, rim_size)
    buffer = jnp.concatenate([before_timed, timed, after_timed], axis=1)
    lane_width = SFT_DEV * NP
    tmpl_local = delay_code.shape[0]
    run_count = span_len // RUN
    code_time = (
        delay_code.reshape(tmpl_local, NQ, SFT_DEV, NP)
        .transpose(0, 2, 1, 3)
        .reshape(tmpl_local, run_count, RUN)
    )
    offsets = code_time[:, :, 0] // NFRAC - MAXD
    run_starts = (jnp.arange(run_count, dtype=jnp.int32) * RUN)[None, :] + offsets + (rim_size - 1)

    def take_segment(start):
        return lax.dynamic_slice_in_dim(buffer, start, RUN + 3, 1)

    segments = jax.vmap(jax.vmap(take_segment))(run_starts)
    fraction = (code_time % NFRAC).astype(jnp.float32) / NFRAC
    coeffs = lagrange(fraction)
    res_time = coeffs[0][:, :, None, :] * segments[:, :, :, 0:RUN]
    for tap_index in range(1, 4):
        res_time = (
            res_time
            + coeffs[tap_index][:, :, None, :] * segments[:, :, :, tap_index : tap_index + RUN]
        )
    resampled = res_time.transpose(0, 2, 1, 3).reshape(tmpl_local, 2, SFT_DEV, NQ, NP)
    resampled = resampled.transpose(0, 1, 3, 2, 4).reshape(tmpl_local, 2, NQ, lane_width)
    weight_a = antenna[:, 0]
    weight_b = antenna[:, 1]
    local_sums = jnp.stack(
        [
            jnp.sum(weight_a * weight_a, axis=(1, 2)),
            jnp.sum(weight_b * weight_b, axis=(1, 2)),
            jnp.sum(weight_a * weight_b, axis=(1, 2)),
        ],
        axis=1,
    )
    totals = lax.psum(local_sums, ("tm", "band"))
    payload = jnp.stack([resampled, antenna], axis=1)
    spectra_out = finish(
        apply_weights(
            lax.all_to_all(
                payload[:, :, :, :, None, :],
                ("tm", "band"),
                split_axis=3,
                concat_axis=4,
                tiled=True,
            )
        )
    )
    out_scale = 1.0 / math.sqrt(sample_total)
    a_real = spectra_out[:, 0, 0] * out_scale
    a_imag = spectra_out[:, 0, 1] * out_scale
    b_real = spectra_out[:, 1, 0] * out_scale
    b_imag = spectra_out[:, 1, 1] * out_scale
    power_a = (totals[:, 0] / sample_total + stat_eps)[:, None, None]
    power_b = (totals[:, 1] / sample_total + stat_eps)[:, None, None]
    cross_ab = (totals[:, 2] / sample_total)[:, None, None]
    det_floor = jnp.maximum(
        power_a * power_b - cross_ab * cross_ab, floor_share * power_a * power_b
    )
    f_stat = (
        power_b * (a_real * a_real + a_imag * a_imag)
        + power_a * (b_real * b_real + b_imag * b_imag)
        - 2.0 * cross_ab * (a_real * b_real + a_imag * b_imag)
    ) / det_floor
    return f_stat[:, :, None, :]


def solution(mesh):
    in_specs = (
        P(None, ("groups", "tm"), "band"),
        P(("groups", "tmpl"), None, ("tm", "band")),
        P(("groups", "tmpl"), None, None, ("tm", "band")),
    )
    out_specs = P(("groups", "tmpl"), None, ("tm", "band"), None)
    return jax.shard_map(
        per_device, mesh=mesh, in_specs=in_specs, out_specs=out_specs, check_vma=False
    )
```

profile of v0, /device:TPU:0, one launch (start us, length us, event | category | flops | bytes accessed | tf_op | source)
XLA Modules:
  0.0 251.6 jit_solution(13160571256986657289)
XLA Ops:
  0.0 1.7 copy.101
  1.7 4.2 %all-to-all-start = ((f32[2,16,1024]{2,0,1:T(2,128)}), f32[2,16,1024]{2,0,1:T(2,128)S(1)}, u32[]{:S(2)}, u32[]{:S(2)}) async-start(f32[2,16,1024]{2,0,1:T(2,128)} %copy.101), calls=%async_computation | async-start | bytes 262144 | tf_op jit(solution)/shard_map/all_to_all | solution.py:108
  6.1 1.8 copy.116
  7.9 1.1 multiply_reduce_fusion.2
  9.0 1.0 copy.99
  14.8 4.0 %collective-permute-start = (f32[2,16,63]{2,1,0:T(8,128)S(1)}, f32[2,16,63]{2,1,0:T(8,128)S(1)}, u32[]{:S(2)}, u32[]{:S(2)}) collective-permute-start(f32[2,16,63]{2,1,0:T(8,128)S(1)} %get-tuple-element.51), channel_id=1, source_target_pairs={{0,2},{2,4},{4,6},{6,8},{8,10},{10,12},{12,14},{1,3},{3,5},{5,7},{... | collective-permute-start | bytes 24200 | tf_op jit(solution)/shard_map/ppermute | solution.py:21
  18.8 1.3 collective-permute-start.1
  21.2 3.2 %collective-permute-done.1 = f32[2,16,63]{2,1,0:T(8,128)S(1)} collective-permute-done((f32[2,16,63]{2,1,0:T(8,128)S(1)}, f32[2,16,63]{2,1,0:T(8,128)S(1)}, u32[]{:S(2)}, u32[]{:S(2)}) %collective-permute-start.1) | collective-permute-done | bytes 8096 | tf_op jit(solution)/shard_map/ppermute | solution.py:21
  25.0 168.8 %while.1 = (s32[]{:T(128)}, f32[2,18400]{1,0:T(2,128)S(1)}, s32[128,2]{1,0:T(8,128)S(1)}, f32[128,2,259]{2,1,0:T(2,128)S(1)}, s32[]{:T(128)}) while((s32[]{:T(128)}, f32[2,18400]{1,0:T(2,128)S(1)}, s32[128,2]{1,0:T(8,128)S(1)}, f32[128,2,259]{2,1,0:T(2,128)S(1)}, s32[]{:T(128)}) %tuple.47), condition=%wide.while_cond, body=%wide.while_body.sunk | while | flops 2 | bytes 6241 | solution.py:140
  28.2 0.7 bitcast_dynamic-update-slice_fusion.2
  32.2 0.7 bitcast_dynamic-update-slice_fusion.2
  34.8 0.7 bitcast_dynamic-update-slice_fusion.2
  36.1 0.7 bitcast_dynamic-update-slice_fusion.2
  38.8 0.7 bitcast_dynamic-update-slice_fusion.2
  42.7 0.7 bitcast_dynamic-update-slice_fusion.2
  193.8 0.9 fusion.214
  196.0 1.0 maximum_bitcast_fusion
  197.0 1.0 copy.117
  198.0 5.8 %all-to-all-start.1 = ((f32[2,2,2,128,1,128]{5,2,0,1,4,3:T(2,128)}), f32[2,2,2,128,1,128]{5,2,0,1,4,3:T(2,128)S(1)}, u32[]{:S(2)}, u32[]{:S(2)}) async-start(f32[2,2,2,128,1,128]{5,2,0,1,4,3:T(2,128)} %copy.117), calls=%async_computation.1 | async-start | bytes 1048576 | tf_op jit(solution)/shard_map/all_to_all | solution.py:167
  203.8 22.1 %psum.7 = f32[2,3]{0,1:T(4,128)S(1)} all-reduce(f32[2,3]{0,1:T(4,128)S(1)} %pad_maximum_fusion.2), channel_id=1, replica_groups=mesh['groups'=2,'tm'=4,'band'=2,'tmpl'=2] {'tm','band'}, use_global_device_ids=true, to_apply=%region_3.4 | all-reduce | flops 6 | bytes 48 | tf_op jit(solution)/shard_map/psum | solution.py:163
  230.8 0.9 copy.123
  231.7 3.7 %all-to-all-start.2 = ((f32[2,2,2,16,8,128]{5,3,1,0,2,4:T(8,128)}), f32[2,2,2,16,8,128]{5,3,1,0,2,4:T(8,128)S(1)}, u32[]{:S(2)}, u32[]{:S(2)}) async-start(f32[2,2,2,16,8,128]{5,3,1,0,2,4:T(8,128)} %copy.123), calls=%async_computation.2 | async-start | bytes 1048576 | tf_op jit(solution)/shard_map/all_to_all | solution.py:90
  236.1 10.6 %all-to-all-done.2 = f32[2,2,2,16,8,128]{5,3,1,0,2,4:T(8,128)S(1)} async-done(((f32[2,2,2,16,8,128]{5,3,1,0,2,4:T(8,128)}), f32[2,2,2,16,8,128]{5,3,1,0,2,4:T(8,128)S(1)}, u32[]{:S(2)}, u32[]{:S(2)}) %all-to-all-start.2) | async-done | bytes 524320 | tf_op jit(solution)/shard_map/all_to_all | solution.py:90
  250.9 0.8 fusion.36
  (461 shorter events, 181.6 us)
Async XLA Ops:
  1.7 9.7 %all-to-all-start = ((f32[2,16,1024]{2,0,1:T(2,128)}), f32[2,16,1024]{2,0,1:T(2,128)S(1)}, u32[]{:S(2)}, u32[]{:S(2)}) async-start(f32[2,16,1024]{2,0,1:T(2,128)} %copy.101), calls=%async_computation | async-start | bytes 262144 | tf_op jit(solution)/shard_map/all_to_all | solution.py:108
  14.8 6.2 %collective-permute-start = (f32[2,16,63]{2,1,0:T(8,128)S(1)}, f32[2,16,63]{2,1,0:T(8,128)S(1)}, u32[]{:S(2)}, u32[]{:S(2)}) collective-permute-start(f32[2,16,63]{2,1,0:T(8,128)S(1)} %get-tuple-element.51), channel_id=1, source_target_pairs={{0,2},{2,4},{4,6},{6,8},{8,10},{10,12},{12,14},{1,3},{3,5},{5,7},{... | collective-permute-start | bytes 24200 | tf_op jit(solution)/shard_map/ppermute | solution.py:21
  18.8 5.6 %collective-permute-start.1 = (f32[2,16,63]{2,1,0:T(8,128)S(1)}, f32[2,16,63]{2,1,0:T(8,128)S(1)}, u32[]{:S(2)}, u32[]{:S(2)}) collective-permute-start(f32[2,16,63]{2,1,0:T(8,128)S(1)} %get-tuple-element.50), channel_id=1, source_target_pairs={{2,0},{4,2},{6,4},{8,6},{10,8},{12,10},{14,12},{3,1},{5,3},{7,5},{... | collective-permute-start | bytes 24200 | tf_op jit(solution)/shard_map/ppermute | solution.py:21
  198.0 29.2 %all-to-all-start.1 = ((f32[2,2,2,128,1,128]{5,2,0,1,4,3:T(2,128)}), f32[2,2,2,128,1,128]{5,2,0,1,4,3:T(2,128)S(1)}, u32[]{:S(2)}, u32[]{:S(2)}) async-start(f32[2,2,2,128,1,128]{5,2,0,1,4,3:T(2,128)} %copy.117), calls=%async_computation.1 | async-start | bytes 1048576 | tf_op jit(solution)/shard_map/all_to_all | solution.py:167
  231.7 15.0 %all-to-all-start.2 = ((f32[2,2,2,16,8,128]{5,3,1,0,2,4:T(8,128)}), f32[2,2,2,16,8,128]{5,3,1,0,2,4:T(8,128)S(1)}, u32[]{:S(2)}, u32[]{:S(2)}) async-start(f32[2,2,2,16,8,128]{5,3,1,0,2,4:T(8,128)} %copy.123), calls=%async_computation.2 | async-start | bytes 1048576 | tf_op jit(solution)/shard_map/all_to_all | solution.py:90
where the time goes:
time: 253 us; the launch traced here: 252 us
  local copies, waits for them, and re-layouts  181 us (72%)
  blocking collectives  22.1 us (9%)
  starting transfers between devices  19 us (8%)
  waiting for transfers between devices  13.8 us (5%)
  matrix products  10.2 us (4%)
  other arithmetic  4.66 us (2%)
    gather x384, local copies, waits for them, and re-layouts  169 us
    psum x1, blocking collectives, per_device(): totals = lax.psum(local_sums, ('tm', 'band'))  22.1 us
    all_to_all x1, waiting for transfers between devices, finish(): lax.all_to_all(packed, ('tm', 'band'), split_axis=4, concat_axis=3, tiled...  10.6 us
    all_to_all x1, starting transfers between devices, per_device(): lax.all_to_all(payload[:, :, :, :, None, :], ('tm', 'band'), split_axis=3...  5.76 us
    ppermute x2, starting transfers between devices, shifted(): return lax.ppermute(value, axis, pairs)  5.3 us
  transfers between devices with their start and end apart: 5, of which 2 were waited for; matrix products, arithmetic and copies ran while one was open for 3% of the time, Pallas kernels for 0%

commit v1 on v0

--- a/solution.py
+++ b/solution.py
@@ -87,7 +87,9 @@
     freq_index = c_grid + owners * (x_grid // NP)
     section_two = rotate(section_two, phase_pair(time_index * freq_index, sample_total, -1.0))
     packed = jnp.stack(section_two, axis=2)
-    turned = lax.all_to_all(packed, ("tm", "band"), split_axis=4, concat_axis=3, tiled=True)
+    pieces = jnp.split(packed, lax.axis_size(("tm", "band")), axis=4)
+    received = lax.all_to_all(jnp.stack(pieces), ("tm", "band"), 0, 0)
+    turned = jnp.concatenate(received, axis=3)
     turned = turned.reshape(turned.shape[0], 2, 2, NQ, lane_width)
     section_three = complex_einsum(
         "abqx,qv->abvx", (turned[:, :, 0], turned[:, :, 1]), dft_table(NQ, -1.0)

time: 253 us -> 258 us (1.020)
  local copies, waits for them, and re-layouts: 181 us -> 185 us
    unnamed x3 -> x10, local copies, waits for them, and re-layouts: 4.44 us -> 8.81 us
where the time goes in v1:
time: 258 us; the launch traced here: 256 us
  local copies, waits for them, and re-layouts  185 us (72%)
  blocking collectives  22.1 us (9%)
  starting transfers between devices  18.8 us (7%)
  waiting for transfers between devices  13.8 us (5%)
  matrix products  10.2 us (4%)
  other arithmetic  5.13 us (2%)
    gather x384, local copies, waits for them, and re-layouts  169 us
    psum x1, blocking collectives, per_device(): totals = lax.psum(local_sums, ('tm', 'band'))  22.1 us
    all_to_all x1, waiting for transfers between devices, finish(): received = lax.all_to_all(jnp.stack(pieces), ('tm', 'band'), 0, 0)  10.6 us
    unnamed x10, local copies, waits for them, and re-layouts  8.81 us
    all_to_all x1, starting transfers between devices, per_device(): lax.all_to_all(payload[:, :, :, :, None, :], ('tm', 'band'), split_axis=3...  5.76 us
    ppermute x2, starting transfers between devices, shifted(): return lax.ppermute(value, axis, pairs)  5.31 us
  transfers between devices with their start and end apart: 5, of which 2 were waited for; matrix products, arithmetic and copies ran while one was open for 3% of the time, Pallas kernels for 0%

profile of v1, /device:TPU:0, one launch (start us, length us, event | category | flops | bytes accessed | tf_op | source)
XLA Modules:
  0.0 256.0 jit_solution(17080846605674349140)
XLA Ops:
  0.0 1.7 copy.122
  1.7 4.2 %all-to-all-start = ((f32[2,16,1024]{2,0,1:T(2,128)}), f32[2,16,1024]{2,0,1:T(2,128)S(1)}, u32[]{:S(2)}, u32[]{:S(2)}) async-start(f32[2,16,1024]{2,0,1:T(2,128)} %copy.122), calls=%async_computation | async-start | bytes 262144 | tf_op jit(solution)/shard_map/all_to_all | solution.py:110
  6.1 1.8 copy.137
  7.9 1.1 multiply_reduce_fusion.2
  9.0 1.0 copy.120
  14.8 4.0 %collective-permute-start = (f32[2,16,63]{2,1,0:T(8,128)S(1)}, f32[2,16,63]{2,1,0:T(8,128)S(1)}, u32[]{:S(2)}, u32[]{:S(2)}) collective-permute-start(f32[2,16,63]{2,1,0:T(8,128)S(1)} %get-tuple-element.59), channel_id=1, source_target_pairs={{0,2},{2,4},{4,6},{6,8},{8,10},{10,12},{12,14},{1,3},{3,5},{5,7},{... | collective-permute-start | bytes 24200 | tf_op jit(solution)/shard_map/ppermute | solution.py:21
  18.8 1.3 collective-permute-start.1
  21.2 3.2 %collective-permute-done.1 = f32[2,16,63]{2,1,0:T(8,128)S(1)} collective-permute-done((f32[2,16,63]{2,1,0:T(8,128)S(1)}, f32[2,16,63]{2,1,0:T(8,128)S(1)}, u32[]{:S(2)}, u32[]{:S(2)}) %collective-permute-start.1) | collective-permute-done | bytes 8096 | tf_op jit(solution)/shard_map/ppermute | solution.py:21
  25.0 168.8 %while.1 = (s32[]{:T(128)}, f32[2,18400]{1,0:T(2,128)S(1)}, s32[128,2]{1,0:T(8,128)S(1)}, f32[128,2,259]{2,1,0:T(2,128)S(1)}, s32[]{:T(128)}) while((s32[]{:T(128)}, f32[2,18400]{1,0:T(2,128)S(1)}, s32[128,2]{1,0:T(8,128)S(1)}, f32[128,2,259]{2,1,0:T(2,128)S(1)}, s32[]{:T(128)}) %tuple.54), condition=%wide.while_cond, body=%wide.while_body.sunk | while | flops 2 | bytes 6241 | solution.py:142
  28.2 0.7 bitcast_dynamic-update-slice_fusion.2
  32.2 0.7 bitcast_dynamic-update-slice_fusion.2
  34.8 0.7 bitcast_dynamic-update-slice_fusion.2
  38.8 0.7 bitcast_dynamic-update-slice_fusion.2
  42.7 0.7 bitcast_dynamic-update-slice_fusion.2
  45.4 0.7 bitcast_dynamic-update-slice_fusion.2
  46.7 0.7 bitcast_dynamic-update-slice_fusion.2
  193.8 0.9 fusion.221
  196.0 1.0 maximum_bitcast_fusion
  197.0 1.0 copy.138
  198.0 5.8 %all-to-all-start.1 = ((f32[2,2,2,128,1,128]{5,2,0,1,4,3:T(2,128)}), f32[2,2,2,128,1,128]{5,2,0,1,4,3:T(2,128)S(1)}, u32[]{:S(2)}, u32[]{:S(2)}) async-start(f32[2,2,2,128,1,128]{5,2,0,1,4,3:T(2,128)} %copy.138), calls=%async_computation.1 | async-start | bytes 1048576 | tf_op jit(solution)/shard_map/all_to_all | solution.py:169
  203.8 22.1 %psum.7 = f32[2,3]{0,1:T(4,128)S(1)} all-reduce(f32[2,3]{0,1:T(4,128)S(1)} %pad_maximum_fusion.2), channel_id=1, replica_groups=mesh['groups'=2,'tm'=4,'band'=2,'tmpl'=2] {'tm','band'}, use_global_device_ids=true, to_apply=%region_3.4 | all-reduce | flops 6 | bytes 48 | tf_op jit(solution)/shard_map/psum | solution.py:165
  236.3 3.5 %all-to-all-start.2 = ((f32[8,2,2,2,16,1,128]{6,4,2,1,3,5,0:T(8,128)}), f32[8,2,2,2,16,1,128]{6,4,2,1,3,5,0:T(8,128)S(1)}, u32[]{:S(2)}, u32[]{:S(2)}) async-start(f32[8,2,2,2,16,1,128]{6,4,2,1,3,5,0:T(8,128)} %constant_dynamic-update-slice_fusion), calls=%async_computation.2 | async-start | bytes 1048576 | tf_op jit(solution)/shard_map/all_to_all | solution.py:91
  240.5 10.6 %all-to-all-done.2 = f32[8,2,2,2,16,1,128]{6,4,2,1,3,5,0:T(8,128)S(1)} async-done(((f32[8,2,2,2,16,1,128]{6,4,2,1,3,5,0:T(8,128)}), f32[8,2,2,2,16,1,128]{6,4,2,1,3,5,0:T(8,128)S(1)}, u32[]{:S(2)}, u32[]{:S(2)}) %all-to-all-start.2) | async-done | bytes 524320 | tf_op jit(solution)/shard_map/all_to_all | solution.py:91
  255.2 0.8 fusion.36
  (468 shorter events, 186.3 us)
Async XLA Ops:
  1.7 9.7 %all-to-all-start = ((f32[2,16,1024]{2,0,1:T(2,128)}), f32[2,16,1024]{2,0,1:T(2,128)S(1)}, u32[]{:S(2)}, u32[]{:S(2)}) async-start(f32[2,16,1024]{2,0,1:T(2,128)} %copy.122), calls=%async_computation | async-start | bytes 262144 | tf_op jit(solution)/shard_map/all_to_all | solution.py:110
  14.8 6.2 %collective-permute-start = (f32[2,16,63]{2,1,0:T(8,128)S(1)}, f32[2,16,63]{2,1,0:T(8,128)S(1)}, u32[]{:S(2)}, u32[]{:S(2)}) collective-permute-start(f32[2,16,63]{2,1,0:T(8,128)S(1)} %get-tuple-element.59), channel_id=1, source_target_pairs={{0,2},{2,4},{4,6},{6,8},{8,10},{10,12},{12,14},{1,3},{3,5},{5,7},{... | collective-permute-start | bytes 24200 | tf_op jit(solution)/shard_map/ppermute | solution.py:21
  18.8 5.6 %collective-permute-start.1 = (f32[2,16,63]{2,1,0:T(8,128)S(1)}, f32[2,16,63]{2,1,0:T(8,128)S(1)}, u32[]{:S(2)}, u32[]{:S(2)}) collective-permute-start(f32[2,16,63]{2,1,0:T(8,128)S(1)} %get-tuple-element.58), channel_id=1, source_target_pairs={{2,0},{4,2},{6,4},{8,6},{10,8},{12,10},{14,12},{3,1},{5,3},{7,5},{... | collective-permute-start | bytes 24200 | tf_op jit(solution)/shard_map/ppermute | solution.py:21
  198.0 29.2 %all-to-all-start.1 = ((f32[2,2,2,128,1,128]{5,2,0,1,4,3:T(2,128)}), f32[2,2,2,128,1,128]{5,2,0,1,4,3:T(2,128)S(1)}, u32[]{:S(2)}, u32[]{:S(2)}) async-start(f32[2,2,2,128,1,128]{5,2,0,1,4,3:T(2,128)} %copy.138), calls=%async_computation.1 | async-start | bytes 1048576 | tf_op jit(solution)/shard_map/all_to_all | solution.py:169
  236.3 14.8 %all-to-all-start.2 = ((f32[8,2,2,2,16,1,128]{6,4,2,1,3,5,0:T(8,128)}), f32[8,2,2,2,16,1,128]{6,4,2,1,3,5,0:T(8,128)S(1)}, u32[]{:S(2)}, u32[]{:S(2)}) async-start(f32[8,2,2,2,16,1,128]{6,4,2,1,3,5,0:T(8,128)} %constant_dynamic-update-slice_fusion), calls=%async_computation.2 | async-start | bytes 1048576 | tf_op jit(solution)/shard_map/all_to_all | solution.py:91
